TPU v7x, 32 devices: a whole 2x2x4 slice. The times are simulated.
32 devices in a mesh: tp: 8 (over y, x, core), dp: 4 (over z).
Axes of the slice: x: 2, y: 2, z: 4, core: 2. Of those that a mesh axis runs over, the one named last changes fastest.
Arguments:
- grad_out: bfloat16 [1792, 8192], P(('dp', 'tp')), may hold values from -6 to 6
- gate_act: bfloat16 [1792, 14336], P('dp', 'tp'), may hold values from -8 to 8
- up_act: bfloat16 [1792, 14336], P('dp', 'tp'), may hold values from -6 to 6
- down_weight: bfloat16 [14336, 8192], P('tp'), may hold values from -0.0625 to 0.0625
Outputs:
- grad_gate: bfloat16 [1792, 14336], P('dp', 'tp')
- grad_up: bfloat16 [1792, 14336], P('dp', 'tp')
- grad_down: bfloat16 [14336, 8192], P(('tp', 'dp'))
All inputs are finite; a program needn't handle non-finite values.
Results may differ from a plain program's by a relative error of at most 0.013.
Values may be sent and summed in bfloat16 or wider, within the bound.
No kernel may reach another device: no remote copies, remote signals or barrier semaphores. Data moves between devices by JAX's collectives and lax.ppermute only.
A program may use at most 128 MiB of HBM per device.

v0:
```python
import math
import jax
import jax.numpy as jnp
from jax import lax
from jax.sharding import PartitionSpec as P


def body(grad_out, gate_act, up_act, down_weight):
    gate_val = gate_act.astype(jnp.float32)
    up_val = up_act.astype(jnp.float32)
    squash = jax.nn.sigmoid(gate_val)
    hidden = (gate_val * squash * up_val).astype(jnp.bfloat16)
    incoming = lax.all_gather(grad_out, "tp", axis=0, tiled=True)
    row_store = incoming
    new_rows = lax.dot_general(
        incoming, down_weight, (((1,), (1,)), ((), ())), preferred_element_type=jnp.float32
    )
    row_store, grad_hidden = (row_store, new_rows)
    weight_part = lax.dot_general(
        hidden, row_store, (((0,), (0,)), ((), ())), preferred_element_type=jnp.float32
    )
    summed = lax.psum_scatter(
        weight_part.astype(jnp.bfloat16), "dp", scatter_dimension=0, tiled=True
    ).astype(jnp.float32)
    grad_gate = (grad_hidden * up_val * squash * (1.0 + gate_val * (1.0 - squash))).astype(
        jnp.bfloat16
    )
    grad_up = (grad_hidden * gate_val * squash).astype(jnp.bfloat16)
    token_total = grad_out.shape[0] * lax.axis_size("tp") * lax.axis_size("dp")
    grad_scale = 1.0 / math.sqrt(token_total)
    grad_down = (summed * grad_scale).astype(jnp.bfloat16)
    return (grad_gate, grad_up, grad_down)


def solution(mesh):
    return jax.shard_map(
        body,
        mesh=mesh,
        in_specs=(P(("dp", "tp"), None), P("dp", "tp"), P("dp", "tp"), P("tp", None)),
        out_specs=(P("dp", "tp"), P("dp", "tp"), P(("tp", "dp"), None)),
        check_vma=False,
    )
```

profile of v0, /device:TPU:16, one launch (start us, length us, event | category | flops | bytes accessed | tf_op | source)
XLA Modules:
  0.0 582.6 jit_solution(4607834574746264727)
XLA Ops:
  7.2 0.0 all-gather.2.cloned.1.call-start
  7.2 0.7 all-gather.2.cloned.1.call-update
  7.9 0.0 reduce-scatter.2.cloned.1.call-start
  7.9 52.8 %all-gather.2.cloned.1.call-done = bf16[448,8192]{1,0:T(8,128)(2,1)} async-done(((bf16[56,8192]{1,0:T(8,128)(2,1)}), bf16[448,8192]{1,0:T(8,128)(2,1)}) %all-gather.2.cloned.1.call-update) | async-done | bytes 7340048 | tf_op jit(solution)/shard_map/all_gather | solution.py:13
  60.8 23.1 %convolution_convert_fusion = bf16[1792,8192]{1,0:T(8,128)(2,1)} fusion(bf16[448,8192]{1,0:T(8,128)(2,1)} %all-gather.2.cloned.1.call-done, bf16[448,1792]{1,0:T(8,128)(2,1)} %param.6, bf16[448,1792]{1,0:T(8,128)(2,1)} %param.5), kind=kOutput, calls=%fused_computation | convolution fusion | flops 13174439936 | bytes 39911424 | tf_op jit(solution)/shard_map/dot_general | solution.py:19
  83.9 0.0 copy-start
  83.9 0.0 copy-start.1
  83.9 0.0 reduce-scatter.2.cloned.1.call-update
  83.9 1.4 copy-done
  85.3 0.5 copy-done.1
  85.8 26.9 %fusion.9 = (bf16[448,1792]{1,0:T(8,128)(2,1)}, bf16[448,1792]{1,0:T(8,128)(2,1)}) fusion(bf16[448,1792]{1,0:T(8,128)(2,1)S(1)} %copy-done, bf16[448,1792]{1,0:T(8,128)(2,1)S(1)} %copy-done.1, bf16[448,8192]{1,0:T(8,128)(2,1)} %all-gather.2.cloned.1.call-done, bf16[1792,8192]{1,0:T(8,128)(2,1)} %param.7), kind=kOutput, calls=%fused_computation.17 | convolution fusion | flops 13165379584 | bytes 43122688 | tf_op jit(solution)/shard_map/dot_general | solution.py:15
  112.7 455.1 %reduce-scatter.2.cloned.1.call-done = bf16[448,8192]{1,0:T(8,128)(2,1)} async-done(((bf16[1792,8192]{1,0:T(8,128)(2,1)}), bf16[448,8192]{1,0:T(8,128)(2,1)}) %reduce-scatter.2.cloned.1.call-update) | async-done | bytes 7340048 | tf_op jit(solution)/shard_map/reduce_scatter | solution.py:22
  567.8 7.9 %multiply_convert_fusion = bf16[448,8192]{1,0:T(8,128)(2,1)} fusion(bf16[448,8192]{1,0:T(8,128)(2,1)} %reduce-scatter.2.cloned.1.call-done), kind=kLoop, calls=%fused_computation.1 | loop fusion | flops 11010048 | bytes 14680064 | tf_op jit(solution)/shard_map/convert_element_type | solution.py:31
Async XLA Ops:
  7.2 53.6 %all-gather.2.cloned.1.call-start = ((), (), s32[]{:S(2)}) async-start(), calls=%async_computation.1 | async-start | bytes 8257536 | tf_op jit(solution)/shard_map/all_gather | solution.py:13
  7.9 559.9 %reduce-scatter.2.cloned.1.call-start = ((), (), s32[]{:S(2)}) async-start(), calls=%async_computation.2 | async-start | bytes 36700160 | tf_op jit(solution)/shard_map/reduce_scatter | solution.py:22
  83.9 1.4 copy-start
  83.9 1.9 copy-start.1
Sparse Core Ops, SparseCore 0:
  9.9 50.8 all-gather.1
  84.0 483.7 reduce-scatter.1
where the time goes:
time: 583 us
  waiting for transfers between devices  509 us (87%)
  matrix products  50 us (9%)
  between operations  14 us (2%)
  other arithmetic  7.93 us (1%)
    reduce_scatter x1, waiting for transfers between devices, body(): lax.psum_scatter(weight_part.astype(jnp.bfloat16), 'dp', scatter_dimensio...  455 us
    all_gather x1, waiting for transfers between devices, body(): incoming = lax.all_gather(grad_out, 'tp', axis=0, tiled=True)  52.8 us
    dot_general x1, matrix products, body(): lax.dot_general(incoming, down_weight, (((1,), (1,)), ((), ())), preferre...  26.9 us
    dot_general x1, matrix products, body(): lax.dot_general(hidden, row_store, (((0,), (0,)), ((), ())), preferred_el...  23.1 us
  transfers between devices with their start and end apart: 2, of which 2 were waited for; matrix products, arithmetic and copies ran while one was open for 5% of the time, Pallas kernels for 0%

commit v1 on v0

--- a/solution.py
+++ b/solution.py
@@ -10,7 +10,9 @@
     up_val = up_act.astype(jnp.float32)
     squash = jax.nn.sigmoid(gate_val)
     hidden = (gate_val * squash * up_val).astype(jnp.bfloat16)
-    incoming = lax.all_gather(grad_out, "tp", axis=0, tiled=True)
+    incoming = jnp.concatenate(
+        lax.all_to_all(jnp.stack([grad_out] * lax.axis_size("tp")), "tp", 0, 0), axis=0
+    )
     row_store = incoming
     new_rows = lax.dot_general(
         incoming, down_weight, (((1,), (1,)), ((), ())), preferred_element_type=jnp.float32

time: 583 us -> 616 us (1.057)
  blocking collectives: 0 us -> 86.6 us
  waiting for transfers between devices: 509 us -> 457 us
    all_to_all x0 -> x1, blocking collectives: none -> 86.6 us  [body(): lax.all_to_all(jnp.stack([grad_out] * lax.axis_size('tp')), 'tp', 0, 0)]
    all_gather x1 -> x0, waiting for transfers between devices: 52.8 us -> none  [body(): incoming = lax.all_gather(grad_out, 'tp', axis=0, tiled=True)]
  transfers between devices with their start and end apart: 2 -> 1, of which waited for: 2 -> 1; matrix products, arithmetic and copies ran while one was open for 5% -> 4% of each run, Pallas kernels for 0% -> 0%
where the time goes in v1:
time: 616 us
  waiting for transfers between devices  457 us (74%)
  blocking collectives  86.6 us (14%)
  matrix products  48.2 us (8%)
  between operations  14.1 us (2%)
  other arithmetic  7.93 us (1%)
    reduce_scatter x1, waiting for transfers between devices, body(): lax.psum_scatter(weight_part.astype(jnp.bfloat16), 'dp', scatter_dimensio...  457 us
    all_to_all x1, blocking collectives, body(): lax.all_to_all(jnp.stack([grad_out] * lax.axis_size('tp')), 'tp', 0, 0)  86.6 us
    dot_general x1, matrix products, body(): lax.dot_general(incoming, down_weight, (((1,), (1,)), ((), ())), preferre...  26.1 us
    dot_general x1, matrix products, body(): lax.dot_general(hidden, row_store, (((0,), (0,)), ((), ())), preferred_el...  22.2 us
  transfers between devices with their start and end apart: 1, of which 1 were waited for; matrix products, arithmetic and copies ran while one was open for 4% of the time, Pallas kernels for 0%

profile of v1, /device:TPU:16, one launch (start us, length us, event | category | flops | bytes accessed | tf_op | source)
XLA Modules:
  0.0 616.0 jit_solution(665777458552893055)
XLA Ops:
  7.2 0.0 reduce-scatter.2.cloned.1.call-start
  7.2 2.0 stack.2
  9.3 0.0 copy-start
  9.3 0.0 copy-start.1
  9.3 86.6 %all_to_all.5 = bf16[8,56,8192]{2,1,0:T(8,128)(2,1)} all-to-all(bf16[8,56,8192]{2,1,0:T(8,128)(2,1)S(1)} %stack.2), channel_id=1, replica_groups=mesh['tp'=8,'dp'=4] {'tp'}, dimensions={0} | all-to-all | bytes 14680064 | tf_op jit(solution)/shard_map/all_to_all | solution.py:14
  95.9 0.0 copy-done
  95.9 0.0 copy-done.1
  95.9 22.2 %convolution_convert_fusion = bf16[1792,8192]{1,0:T(8,128)(2,1)} fusion(bf16[448,8192]{1,0:T(8,128)(2,1)} %bitcast.4, bf16[448,1792]{1,0:T(8,128)(2,1)S(1)} %copy-done.1, bf16[448,1792]{1,0:T(8,128)(2,1)S(1)} %copy-done), kind=kOutput, calls=%fused_computation | convolution fusion | flops 13174439936 | bytes 39911424 | tf_op jit(solution)/shard_map/dot_general | solution.py:21
  118.1 0.0 reduce-scatter.2.cloned.1.call-update
  118.1 26.1 %fusion.9 = (bf16[448,1792]{1,0:T(8,128)(2,1)}, bf16[448,1792]{1,0:T(8,128)(2,1)}) fusion(bf16[448,1792]{1,0:T(8,128)(2,1)S(1)} %copy-done, bf16[448,1792]{1,0:T(8,128)(2,1)S(1)} %copy-done.1, bf16[448,8192]{1,0:T(8,128)(2,1)} %bitcast.5, bf16[1792,8192]{1,0:T(8,128)(2,1)} %param.7), kind=kOutput, calls=%fused_computation.17 | convolution fusion | flops 13165379584 | bytes 43122688 | tf_op jit(solution)/shard_map/dot_general | solution.py:17
  144.2 457.1 %reduce-scatter.2.cloned.1.call-done = bf16[448,8192]{1,0:T(8,128)(2,1)} async-done(((bf16[1792,8192]{1,0:T(8,128)(2,1)}), bf16[448,8192]{1,0:T(8,128)(2,1)}) %reduce-scatter.2.cloned.1.call-update) | async-done | bytes 7340048 | tf_op jit(solution)/shard_map/reduce_scatter | solution.py:24
  601.2 7.9 %multiply_convert_fusion = bf16[448,8192]{1,0:T(8,128)(2,1)} fusion(bf16[448,8192]{1,0:T(8,128)(2,1)} %reduce-scatter.2.cloned.1.call-done), kind=kLoop, calls=%fused_computation.1 | loop fusion | flops 11010048 | bytes 14680064 | tf_op jit(solution)/shard_map/convert_element_type | solution.py:33
Async XLA Ops:
  7.2 594.1 %reduce-scatter.2.cloned.1.call-start = ((), (), s32[]{:S(2)}) async-start(), calls=%async_computation.2 | async-start | bytes 36700160 | tf_op jit(solution)/shard_map/reduce_scatter | solution.py:24
  9.3 86.7 %copy-start = (bf16[448,1792]{1,0:T(8,128)(2,1)S(1)}, bf16[448,1792]{1,0:T(8,128)(2,1)}, u32[]{:S(2)}) copy-start(bf16[448,1792]{1,0:T(8,128)(2,1)} %param.5) | copy-start | bytes 4816900
  9.3 86.6 %copy-start.1 = (bf16[448,1792]{1,0:T(8,128)(2,1)S(1)}, bf16[448,1792]{1,0:T(8,128)(2,1)}, u32[]{:S(2)}) copy-start(bf16[448,1792]{1,0:T(8,128)(2,1)} %param.6) | copy-start | bytes 4816900
Sparse Core Ops, SparseCore 0:
  118.2 482.9 reduce-scatter.1
